TPU v7x, 512 devices: a whole 4x4x16 slice. The times are simulated.
512 devices in a mesh: src: 16 (over z), tile: 8 (over x, core), gauge: 4 (over y).
Axes of the slice: x: 4, y: 4, z: 16, core: 2. Of those that a mesh axis runs over, the one named last changes fastest.
Arguments:
- responses: float32 [512, 2, 4, 128, 256], P(('src', 'tile'), None, 'gauge'), may hold values from -0.1875 to 0.1875
- footprint: int32 [512, 2], P(('src', 'tile')), may hold values from 0 to 15, all different within a row; in each aligned block of 4 rows (0 to 3, 4 to 7, ...) at most 2 rows name the same one
- theta_start: float32 [512, 8, 128], P(('src', 'tile')), may hold values from -4 to 4
- observed: float32 [128, 4, 8, 256], P(('src', 'tile'), 'gauge'), may hold values from -6 to 6
Outputs:
- theta: float32 [512, 8, 128], P(('src', 'tile'))
- misfit: float32 [128, 4, 8, 256], P(('src', 'tile'), 'gauge')
Inputs may be any that keep to these rules, and one draw needn't show every extreme that they name: `footprint`: each source's 2 entries differ. Among the 4 sources of one src and tile index, no value is named more than 2 times, a bound that some block reaches.
All inputs are finite; a program needn't handle non-finite values.
Results may differ from a plain program's by a relative error of at most 0.00017.
Values sent between devices are 32-bit elements; how exact they have to be, the bound alone decides.
A program may use at most 64 MiB of HBM per device.

v0:
```python
import jax
import jax.numpy as jnp
from jax import lax
from jax.sharding import PartitionSpec as P

GN_STEPS = 2
CG_ITERS = 2
damping = 0.1
highest = lax.Precision.HIGHEST


def local(responses, footprint, theta_start, observed):
    n_src = lax.axis_size("src")
    n_gauge = lax.axis_size("gauge")
    src_dev, foot, wins, width, length = responses.shape
    count = src_dev * foot
    blocks = responses.reshape(count, wins, width, length)
    target = footprint.reshape(count)
    dest_hot = (target[:, None] == jnp.arange(n_src, dtype=jnp.int32)[None, :]).astype(jnp.float32)
    capacity = max(2, -(-count // n_src))
    slots = n_src * capacity
    rank = jnp.sum(dest_hot * (jnp.cumsum(dest_hot, axis=0) - 1.0), axis=1).astype(jnp.int32)
    slot_of = target * capacity + rank
    slot_hot = (slot_of[:, None] == jnp.arange(slots, dtype=jnp.int32)[None, :]).astype(jnp.float32)
    observed_here = observed[0]
    packed_blocks = jnp.einsum("bq,bwkl->qwkl", slot_hot, blocks, precision=highest)
    received_blocks = lax.all_to_all(packed_blocks, "src", split_axis=0, concat_axis=0, tiled=True)

    def forward(values):
        spread = jnp.repeat(values, foot, axis=0)
        packed = jnp.einsum("bq,bek->qek", slot_hot, spread, precision=highest)
        arrived = lax.all_to_all(packed, "src", split_axis=0, concat_axis=0, tiled=True)
        return jnp.einsum("qek,qwkl->wel", arrived, received_blocks, precision=highest)

    def adjoint(field):
        backward = jnp.einsum("wel,qwkl->qek", field, received_blocks, precision=highest)
        returned = lax.all_to_all(backward, "src", split_axis=0, concat_axis=0, tiled=True)
        per_block = jnp.einsum("bq,qek->bek", slot_hot, returned, precision=highest)
        summed = jnp.sum(
            per_block.reshape(src_dev, foot, per_block.shape[1], per_block.shape[2]), axis=1
        )
        return lax.psum(summed, "gauge")

    theta = theta_start
    misfit = jnp.zeros_like(observed_here)
    for outer in range(GN_STEPS):
        coef = jax.nn.softplus(theta)
        slope = jax.nn.sigmoid(theta)
        misfit = forward(coef) - observed_here
        grad = slope * adjoint(misfit) + damping * theta
        update = jnp.zeros_like(theta)
        res = -grad
        direction = res
        norm_now = lax.psum(jnp.sum(res * res, axis=(0, 2)), ("src", "tile"))
        for inner in range(CG_ITERS):
            image = forward(slope * direction)
            norm_next = norm_now
            local_curv = (
                jnp.sum(image * image, axis=(0, 2))
                + damping * jnp.sum(direction * direction, axis=(0, 2)) / n_gauge
            )
            curv = lax.psum(local_curv, ("src", "tile", "gauge"))
            alpha = norm_now / curv
            applied = slope * adjoint(image) + damping * direction
            update = update + alpha[None, :, None] * direction
            res = res - alpha[None, :, None] * applied
            if inner + 1 < CG_ITERS:
                norm_next = lax.psum(jnp.sum(res * res, axis=(0, 2)), ("src", "tile"))
            if inner + 1 < CG_ITERS:
                direction = res + (norm_next / norm_now)[None, :, None] * direction
                norm_now = norm_next
        theta = theta + update
    return (theta, misfit[None])


def solution(mesh):
    in_specs = (
        P(("src", "tile"), None, "gauge", None, None),
        P(("src", "tile"), None),
        P(("src", "tile"), None, None),
        P(("src", "tile"), "gauge", None, None),
    )
    out_specs = (P(("src", "tile"), None, None), P(("src", "tile"), "gauge", None, None))
    return jax.shard_map(local, mesh=mesh, in_specs=in_specs, out_specs=out_specs, check_vma=False)
```

profile of v0, /device:TPU:1, one launch (start us, length us, event | category | flops | bytes accessed | tf_op | source)
XLA Modules:
  0.0 1926.5 jit_solution(504612940981126562)
XLA Ops:
  0.6 0.9 copy.83
  1.9 0.7 compare_select_fusion.1
  2.6 0.3 fusion.105
  3.0 0.7 copy.92
  3.7 15.7 all-to-all-start.1
  19.4 2.1 convolution_bitcast_fusion
  21.5 4.4 copy.85
  25.9 5.5 all-to-all-done.1
  31.4 6.7 all-to-all-start
  38.4 181.6 %all-to-all-done = f32[32,1,128,256]{3,2,1,0:T(8,128)} async-done(((f32[32,1,128,256]{3,2,1,0:T(8,128)}), f32[32,1,128,256]{3,2,1,0:T(8,128)}, u32[]{:S(2)}, u32[]{:S(2)}) %all-to-all-start) | async-done | bytes 4194336 | tf_op jit(solution)/shard_map/all_to_all | solution.py:27
  220.0 6.8 fusion.48
  226.8 12.1 fusion.30
  239.1 22.9 %all_to_all.55 = f32[32,8,128]{2,1,0:T(8,128)S(1)} all-to-all(f32[32,8,128]{2,1,0:T(8,128)S(1)} %copy.94), channel_id=1, replica_groups=mesh['src'=16,'tile'=8,'gauge'=4] {'src'}, dimensions={0} | all-to-all | bytes 262144 | tf_op jit(solution)/shard_map/all_to_all | solution.py:37
  262.3 13.7 psum.84
  276.2 0.3 fusion.102
  276.6 18.1 all_to_all.56
  294.9 6.9 fusion.88
  301.8 12.1 fusion.33
  313.9 0.9 copy.99
  314.8 4.0 all-to-all-start.4
  318.8 252.9 %psum.85 = f32[8]{0:T(128)S(1)} all-reduce(f32[8]{0:T(128)S(1)} %get-tuple-element.16), channel_id=1, replica_groups=mesh['src'=16,'tile'=8,'gauge'=4] {'src','tile'}, use_global_device_ids=true, to_apply=%region_5.6 | all-reduce | flops 8 | bytes 64 | tf_op jit(solution)/shard_map/psum | solution.py:54
  571.7 99.7 %psum.86 = f32[8]{0:T(128)S(1)} all-reduce(f32[8]{0:T(128)S(1)} %multiply_add_fusion.7), channel_id=1, replica_groups=mesh['src'=16,'tile'=8,'gauge'=4] {'src','tile','gauge'}, use_global_device_ids=true, to_apply=%region_7.8 | all-reduce | flops 8 | bytes 64 | tf_op jit(solution)/shard_map/psum | solution.py:62
  671.7 13.2 psum.87
  685.1 250.6 %psum.88 = f32[8]{0:T(128)S(1)} all-reduce(f32[8]{0:T(128)S(1)} %get-tuple-element.14), channel_id=1, replica_groups=mesh['src'=16,'tile'=8,'gauge'=4] {'src','tile'}, use_global_device_ids=true, to_apply=%region_11.12 | all-reduce | flops 8 | bytes 64 | tf_op jit(solution)/shard_map/psum | solution.py:68
  935.9 0.3 fusion.99
  936.3 22.0 %all_to_all.57 = f32[32,8,128]{2,1,0:T(8,128)S(1)} all-to-all(f32[32,8,128]{2,1,0:T(8,128)S(1)} %copy.101), channel_id=1, replica_groups=mesh['src'=16,'tile'=8,'gauge'=4] {'src'}, dimensions={0} | all-to-all | bytes 262144 | tf_op jit(solution)/shard_map/all_to_all | solution.py:32
  958.6 6.5 fusion.72
  965.1 101.3 %psum.89 = f32[8]{0:T(128)S(1)} all-reduce(f32[8]{0:T(128)S(1)} %multiply_add_fusion.6), channel_id=1, replica_groups=mesh['src'=16,'tile'=8,'gauge'=4] {'src','tile','gauge'}, use_global_device_ids=true, to_apply=%region_14.15 | all-reduce | flops 8 | bytes 64 | tf_op jit(solution)/shard_map/psum | solution.py:62
  1066.5 0.3 fusion.97
  1067.0 17.0 all_to_all.58
  1084.3 6.8 fusion.60
  1091.1 12.1 fusion.36
  1103.4 17.8 all_to_all.59
  1121.4 13.2 psum.90
  1134.8 0.3 fusion.94
  1135.2 17.3 all_to_all.60
  1152.8 6.9 fusion.86
  1159.8 12.1 fusion.39
  1171.9 0.9 copy.110
  1172.7 4.0 all-to-all-start.9
  1176.7 253.3 %psum.91 = f32[8]{0:T(128)S(1)} all-reduce(f32[8]{0:T(128)S(1)} %get-tuple-element.10), channel_id=1, replica_groups=mesh['src'=16,'tile'=8,'gauge'=4] {'src','tile'}, use_global_device_ids=true, to_apply=%region_18.19 | all-reduce | flops 8 | bytes 64 | tf_op jit(solution)/shard_map/psum | solution.py:54
  1430.1 100.1 %psum.92 = f32[8]{0:T(128)S(1)} all-reduce(f32[8]{0:T(128)S(1)} %multiply_add_fusion.5), channel_id=1, replica_groups=mesh['src'=16,'tile'=8,'gauge'=4] {'src','tile','gauge'}, use_global_device_ids=true, to_apply=%region_20.21 | all-reduce | flops 8 | bytes 64 | tf_op jit(solution)/shard_map/psum | solution.py:62
  1530.5 13.2 psum.93
  1543.9 250.6 %psum.94 = f32[8]{0:T(128)S(1)} all-reduce(f32[8]{0:T(128)S(1)} %get-tuple-element.8), channel_id=1, replica_groups=mesh['src'=16,'tile'=8,'gauge'=4] {'src','tile'}, use_global_device_ids=true, to_apply=%region_24.25 | all-reduce | flops 8 | bytes 64 | tf_op jit(solution)/shard_map/psum | solution.py:68
  1795.1 22.1 %all_to_all.61 = f32[32,8,128]{2,1,0:T(8,128)S(1)} all-to-all(f32[32,8,128]{2,1,0:T(8,128)S(1)} %copy.112), channel_id=1, replica_groups=mesh['src'=16,'tile'=8,'gauge'=4] {'src'}, dimensions={0} | all-to-all | bytes 262144 | tf_op jit(solution)/shard_map/all_to_all | solution.py:32
  1817.5 6.5 fusion.69
  1824.0 101.3 %psum.95 = f32[8]{0:T(128)S(1)} all-reduce(f32[8]{0:T(128)S(1)} %multiply_add_fusion.4), channel_id=1, replica_groups=mesh['src'=16,'tile'=8,'gauge'=4] {'src','tile','gauge'}, use_global_device_ids=true, to_apply=%region_27.28 | all-reduce | flops 8 | bytes 64 | tf_op jit(solution)/shard_map/psum | solution.py:62
  1925.4 0.6 copy.114
  (63 shorter events, 5.7 us)
Async XLA Ops:
  0.6 18.8 copy-start
  3.7 27.7 %all-to-all-start.1 = ((f32[32,8,128]{2,1,0:T(8,128)}), f32[32,8,128]{2,1,0:T(8,128)S(1)}, u32[]{:S(2)}, u32[]{:S(2)}) async-start(f32[32,8,128]{2,1,0:T(8,128)} %copy.92), calls=%async_computation.1 | async-start | bytes 262144 | tf_op jit(solution)/shard_map/all_to_all | solution.py:32
  25.9 194.0 %copy-start.2 = (f32[1,1,8,256]{3,2,1,0:T(8,128)S(1)}, f32[1,1,8,256]{3,2,1,0:T(8,128)}, u32[]{:S(2)}) copy-start(f32[1,1,8,256]{3,2,1,0:T(8,128)} %param.7) | copy-start | bytes 24580
  31.4 188.6 %all-to-all-start = ((f32[32,1,128,256]{3,2,1,0:T(8,128)}), f32[32,1,128,256]{3,2,1,0:T(8,128)}, u32[]{:S(2)}, u32[]{:S(2)}) async-start(f32[32,1,128,256]{3,2,1,0:T(8,128)} %copy.85), calls=%async_computation | async-start | bytes 8388608 | tf_op jit(solution)/shard_map/all_to_all | solution.py:27
  38.4 237.6 %copy-start.1 = (f32[4,8,128]{2,1,0:T(8,128)S(1)}, f32[4,8,128]{2,1,0:T(8,128)}, u32[]{:S(2)}) copy-start(f32[4,8,128]{2,1,0:T(8,128)} %param.6) | copy-start | bytes 49156
  314.8 356.6 %all-to-all-start.4 = ((f32[32,8,128]{2,1,0:T(8,128)}), f32[32,8,128]{2,1,0:T(8,128)S(1)}, u32[]{:S(2)}, u32[]{:S(2)}) async-start(f32[32,8,128]{2,1,0:T(8,128)} %copy.99), calls=%async_computation.4 | async-start | bytes 262144 | tf_op jit(solution)/shard_map/all_to_all | solution.py:37
  1091.1 68.7 %copy-start.3 = (f32[1,8,256]{2,1,0:T(8,128)}, f32[1,8,256]{2,1,0:T(8,128)S(1)}, u32[]{:S(2)}) copy-start(f32[1,8,256]{2,1,0:T(8,128)S(1)} %fusion.60) | copy-start | bytes 24580
  1172.7 357.5 %all-to-all-start.9 = ((f32[32,8,128]{2,1,0:T(8,128)}), f32[32,8,128]{2,1,0:T(8,128)S(1)}, u32[]{:S(2)}, u32[]{:S(2)}) async-start(f32[32,8,128]{2,1,0:T(8,128)} %copy.110), calls=%async_computation.9 | async-start | bytes 262144 | tf_op jit(solution)/shard_map/all_to_all | solution.py:37
where the time goes:
time: 1930 us
  blocking collectives  1600 us (83%)
  waiting for transfers between devices  187 us (10%)
  matrix products  93.6 us (5%)
  starting transfers between devices  30.5 us (2%)
    psum x2, blocking collectives, local(): norm_now = lax.psum(jnp.sum(res * res, axis=(0, 2)), ('src', 'tile'))  506 us
    psum x2, blocking collectives, local(): norm_next = lax.psum(jnp.sum(res * res, axis=(0, 2)), ('src', 'tile'))  501 us
    psum x4, blocking collectives, local(): curv = lax.psum(local_curv, ('src', 'tile', 'gauge'))  402 us
    all_to_all x1, waiting for transfers between devices, local(): lax.all_to_all(packed_blocks, 'src', split_axis=0, concat_axis=0, tiled=T...  182 us
    all_to_all x5, blocking collectives, forward(): lax.all_to_all(packed, 'src', split_axis=0, concat_axis=0, tiled=True)  96.6 us
    psum x4, blocking collectives, adjoint(): return lax.psum(summed, 'gauge')  53.3 us
    dot_general x4, matrix products, adjoint(): jnp.einsum('wel,qwkl->qek', field, received_blocks, precision=highest)  48.3 us
    all_to_all x2, blocking collectives, adjoint(): lax.all_to_all(backward, 'src', split_axis=0, concat_axis=0, tiled=True)  40.7 us
  transfers between devices with their start and end apart: 4, of which 2 were waited for; matrix products, arithmetic and copies ran while one was open for 0% of the time, Pallas kernels for 0%

commit v1 on v0

--- a/solution.py
+++ b/solution.py
@@ -51,7 +51,7 @@
         update = jnp.zeros_like(theta)
         res = -grad
         direction = res
-        norm_now = lax.psum(jnp.sum(res * res, axis=(0, 2)), ("src", "tile"))
+        norm_now = lax.psum(lax.psum(jnp.sum(res * res, axis=(0, 2)), "src"), "tile")
         for inner in range(CG_ITERS):
             image = forward(slope * direction)
             norm_next = norm_now

time: 1930 us -> 1520 us (0.79)
  blocking collectives: 1600 us -> 1190 us
    psum x2 -> x4, blocking collectives: 506 us -> 97.9 us  [the longest x2 49.8 us: local(): lax.psum(jnp.sum(res * res, axis=(0, 2)), 'src')]
where the time goes in v1:
time: 1520 us; the launch traced here: 1510 us
  blocking collectives  1190 us (78%)
  waiting for transfers between devices  187 us (12%)
  matrix products  93.6 us (6%)
  starting transfers between devices  30.5 us (2%)
    psum x2, blocking collectives, local(): norm_next = lax.psum(jnp.sum(res * res, axis=(0, 2)), ('src', 'tile'))  501 us
    psum x4, blocking collectives, local(): curv = lax.psum(local_curv, ('src', 'tile', 'gauge'))  402 us
    all_to_all x1, waiting for transfers between devices, local(): lax.all_to_all(packed_blocks, 'src', split_axis=0, concat_axis=0, tiled=T...  182 us
    all_to_all x5, blocking collectives, forward(): lax.all_to_all(packed, 'src', split_axis=0, concat_axis=0, tiled=True)  93.9 us
    psum x4, blocking collectives, adjoint(): return lax.psum(summed, 'gauge')  50.2 us
    psum x2, blocking collectives, local(): lax.psum(jnp.sum(res * res, axis=(0, 2)), 'src')  49.8 us
    dot_general x4, matrix products, adjoint(): jnp.einsum('wel,qwkl->qek', field, received_blocks, precision=highest)  48.3 us
    psum x2, blocking collectives, local(): lax.psum(lax.psum(jnp.sum(res * res, axis=(0, 2)), 'src'), 'tile')  48.1 us
  transfers between devices with their start and end apart: 4, of which 2 were waited for; matrix products, arithmetic and copies ran while one was open for 0% of the time, Pallas kernels for 0%

profile of v1, /device:TPU:1, one launch (start us, length us, event | category | flops | bytes accessed | tf_op | source)
XLA Modules:
  0.0 1512.1 jit_solution(8875483739247706153)
XLA Ops:
  0.6 0.9 copy.83
  1.9 0.7 compare_select_fusion.1
  2.6 0.3 fusion.105
  3.0 0.7 copy.92
  3.7 15.7 %all-to-all-start.1 = ((f32[32,8,128]{2,1,0:T(8,128)}), f32[32,8,128]{2,1,0:T(8,128)S(1)}, u32[]{:S(2)}, u32[]{:S(2)}) async-start(f32[32,8,128]{2,1,0:T(8,128)} %copy.92), calls=%async_computation.1 | async-start | bytes 262144 | tf_op jit(solution)/shard_map/all_to_all | solution.py:32
  19.4 2.1 convolution_bitcast_fusion
  21.5 4.4 copy.85
  25.9 5.5 all-to-all-done.1
  31.4 6.7 all-to-all-start
  38.4 181.6 %all-to-all-done = f32[32,1,128,256]{3,2,1,0:T(8,128)} async-done(((f32[32,1,128,256]{3,2,1,0:T(8,128)}), f32[32,1,128,256]{3,2,1,0:T(8,128)}, u32[]{:S(2)}, u32[]{:S(2)}) %all-to-all-start) | async-done | bytes 4194336 | tf_op jit(solution)/shard_map/all_to_all | solution.py:27
  220.0 6.8 fusion.48
  226.8 12.1 fusion.30
  239.1 22.9 %all_to_all.55 = f32[32,8,128]{2,1,0:T(8,128)S(1)} all-to-all(f32[32,8,128]{2,1,0:T(8,128)S(1)} %copy.94), channel_id=1, replica_groups=mesh['src'=16,'tile'=8,'gauge'=4] {'src'}, dimensions={0} | all-to-all | bytes 262144 | tf_op jit(solution)/shard_map/all_to_all | solution.py:37
  262.3 13.7 psum.98
  276.6 18.1 %all_to_all.56 = f32[32,8,128]{2,1,0:T(8,128)S(1)} all-to-all(f32[32,8,128]{2,1,0:T(8,128)S(1)} %copy.97), channel_id=1, replica_groups=mesh['src'=16,'tile'=8,'gauge'=4] {'src'}, dimensions={0} | all-to-all | bytes 262144 | tf_op jit(solution)/shard_map/all_to_all | solution.py:32
  294.9 6.9 fusion.88
  301.8 12.1 fusion.33
  313.9 0.9 copy.99
  314.8 4.0 all-to-all-start.4
  318.8 25.1 %psum.99 = f32[8]{0:T(128)S(1)} all-reduce(f32[8]{0:T(128)S(1)} %get-tuple-element.16), channel_id=1, replica_groups=mesh['src'=16,'tile'=8,'gauge'=4] {'src'}, use_global_device_ids=true, to_apply=%region_5.6 | all-reduce | flops 8 | bytes 64 | tf_op jit(solution)/shard_map/psum | solution.py:54
  343.9 23.4 %psum.100 = f32[8]{0:T(128)S(1)} all-reduce(f32[8]{0:T(128)S(1)} %psum.99), channel_id=1, replica_groups=mesh['src'=16,'tile'=8,'gauge'=4] {'tile'}, use_global_device_ids=true, to_apply=%region_6.7 | all-reduce | flops 8 | bytes 64 | tf_op jit(solution)/shard_map/psum | solution.py:54
  367.3 99.8 %psum.101 = f32[8]{0:T(128)S(1)} all-reduce(f32[8]{0:T(128)S(1)} %multiply_add_fusion.7), channel_id=1, replica_groups=mesh['src'=16,'tile'=8,'gauge'=4] {'src','tile','gauge'}, use_global_device_ids=true, to_apply=%region_8.9 | all-reduce | flops 8 | bytes 64 | tf_op jit(solution)/shard_map/psum | solution.py:62
  467.4 11.6 psum.102
  479.2 250.6 %psum.103 = f32[8]{0:T(128)S(1)} all-reduce(f32[8]{0:T(128)S(1)} %get-tuple-element.14), channel_id=1, replica_groups=mesh['src'=16,'tile'=8,'gauge'=4] {'src','tile'}, use_global_device_ids=true, to_apply=%region_12.13 | all-reduce | flops 8 | bytes 64 | tf_op jit(solution)/shard_map/psum | solution.py:68
  730.5 20.7 %all_to_all.57 = f32[32,8,128]{2,1,0:T(8,128)S(1)} all-to-all(f32[32,8,128]{2,1,0:T(8,128)S(1)} %copy.101), channel_id=1, replica_groups=mesh['src'=16,'tile'=8,'gauge'=4] {'src'}, dimensions={0} | all-to-all | bytes 262144 | tf_op jit(solution)/shard_map/all_to_all | solution.py:32
  751.4 6.5 fusion.72
  757.9 101.3 %psum.104 = f32[8]{0:T(128)S(1)} all-reduce(f32[8]{0:T(128)S(1)} %multiply_add_fusion.6), channel_id=1, replica_groups=mesh['src'=16,'tile'=8,'gauge'=4] {'src','tile','gauge'}, use_global_device_ids=true, to_apply=%region_15.16 | all-reduce | flops 8 | bytes 64 | tf_op jit(solution)/shard_map/psum | solution.py:62
  859.3 0.3 fusion.97
  859.7 17.0 %all_to_all.58 = f32[32,8,128]{2,1,0:T(8,128)S(1)} all-to-all(f32[32,8,128]{2,1,0:T(8,128)S(1)} %copy.104), channel_id=1, replica_groups=mesh['src'=16,'tile'=8,'gauge'=4] {'src'}, dimensions={0} | all-to-all | bytes 262144 | tf_op jit(solution)/shard_map/all_to_all | solution.py:32
  877.0 6.8 fusion.60
  883.9 12.1 fusion.36
  896.2 17.8 %all_to_all.59 = f32[32,8,128]{2,1,0:T(8,128)S(1)} all-to-all(f32[32,8,128]{2,1,0:T(8,128)S(1)} %copy.106), channel_id=1, replica_groups=mesh['src'=16,'tile'=8,'gauge'=4] {'src'}, dimensions={0} | all-to-all | bytes 262144 | tf_op jit(solution)/shard_map/all_to_all | solution.py:37
  914.2 13.2 psum.105
  927.6 0.3 fusion.94
  928.0 17.3 %all_to_all.60 = f32[32,8,128]{2,1,0:T(8,128)S(1)} all-to-all(f32[32,8,128]{2,1,0:T(8,128)S(1)} %copy.108), channel_id=1, replica_groups=mesh['src'=16,'tile'=8,'gauge'=4] {'src'}, dimensions={0} | all-to-all | bytes 262144 | tf_op jit(solution)/shard_map/all_to_all | solution.py:32
  945.6 6.9 fusion.86
  952.6 12.1 fusion.39
  964.7 0.9 copy.110
  965.5 4.0 all-to-all-start.9
  969.5 24.7 %psum.106 = f32[8]{0:T(128)S(1)} all-reduce(f32[8]{0:T(128)S(1)} %get-tuple-element.10), channel_id=1, replica_groups=mesh['src'=16,'tile'=8,'gauge'=4] {'src'}, use_global_device_ids=true, to_apply=%region_19.20 | all-reduce | flops 8 | bytes 64 | tf_op jit(solution)/shard_map/psum | solution.py:54
  994.2 24.7 %psum.107 = f32[8]{0:T(128)S(1)} all-reduce(f32[8]{0:T(128)S(1)} %psum.106), channel_id=1, replica_groups=mesh['src'=16,'tile'=8,'gauge'=4] {'tile'}, use_global_device_ids=true, to_apply=%region_20.21 | all-reduce | flops 8 | bytes 64 | tf_op jit(solution)/shard_map/psum | solution.py:54
  1019.0 99.8 %psum.108 = f32[8]{0:T(128)S(1)} all-reduce(f32[8]{0:T(128)S(1)} %multiply_add_fusion.5), channel_id=1, replica_groups=mesh['src'=16,'tile'=8,'gauge'=4] {'src','tile','gauge'}, use_global_device_ids=true, to_apply=%region_22.23 | all-reduce | flops 8 | bytes 64 | tf_op jit(solution)/shard_map/psum | solution.py:62
  1119.0 11.6 psum.109
  1130.8 250.6 %psum.110 = f32[8]{0:T(128)S(1)} all-reduce(f32[8]{0:T(128)S(1)} %get-tuple-element.8), channel_id=1, replica_groups=mesh['src'=16,'tile'=8,'gauge'=4] {'src','tile'}, use_global_device_ids=true, to_apply=%region_26.27 | all-reduce | flops 8 | bytes 64 | tf_op jit(solution)/shard_map/psum | solution.py:68
  1382.1 20.7 %all_to_all.61 = f32[32,8,128]{2,1,0:T(8,128)S(1)} all-to-all(f32[32,8,128]{2,1,0:T(8,128)S(1)} %copy.112), channel_id=1, replica_groups=mesh['src'=16,'tile'=8,'gauge'=4] {'src'}, dimensions={0} | all-to-all | bytes 262144 | tf_op jit(solution)/shard_map/all_to_all | solution.py:32
  1403.1 6.5 fusion.69
  1409.6 101.3 %psum.111 = f32[8]{0:T(128)S(1)} all-reduce(f32[8]{0:T(128)S(1)} %multiply_add_fusion.4), channel_id=1, replica_groups=mesh['src'=16,'tile'=8,'gauge'=4] {'src','tile','gauge'}, use_global_device_ids=true, to_apply=%region_29.30 | all-reduce | flops 8 | bytes 64 | tf_op jit(solution)/shard_map/psum | solution.py:62
  1511.0 0.6 copy.114
  (65 shorter events, 6.3 us)
Async XLA Ops:
  0.6 18.8 %copy-start = (f32[4,2,1,128,256]{4,3,2,1,0:T(8,128)S(1)}, f32[4,2,1,128,256]{4,3,2,1,0:T(8,128)}, u32[]{:S(2)}) copy-start(f32[4,2,1,128,256]{4,3,2,1,0:T(8,128)} %param.4) | copy-start | bytes 3145732
  3.7 27.7 %all-to-all-start.1 = ((f32[32,8,128]{2,1,0:T(8,128)}), f32[32,8,128]{2,1,0:T(8,128)S(1)}, u32[]{:S(2)}, u32[]{:S(2)}) async-start(f32[32,8,128]{2,1,0:T(8,128)} %copy.92), calls=%async_computation.1 | async-start | bytes 262144 | tf_op jit(solution)/shard_map/all_to_all | solution.py:32
  25.9 194.0 %copy-start.2 = (f32[1,1,8,256]{3,2,1,0:T(8,128)S(1)}, f32[1,1,8,256]{3,2,1,0:T(8,128)}, u32[]{:S(2)}) copy-start(f32[1,1,8,256]{3,2,1,0:T(8,128)} %param.7) | copy-start | bytes 24580
  31.4 188.6 %all-to-all-start = ((f32[32,1,128,256]{3,2,1,0:T(8,128)}), f32[32,1,128,256]{3,2,1,0:T(8,128)}, u32[]{:S(2)}, u32[]{:S(2)}) async-start(f32[32,1,128,256]{3,2,1,0:T(8,128)} %copy.85), calls=%async_computation | async-start | bytes 8388608 | tf_op jit(solution)/shard_map/all_to_all | solution.py:27
  38.4 237.6 %copy-start.1 = (f32[4,8,128]{2,1,0:T(8,128)S(1)}, f32[4,8,128]{2,1,0:T(8,128)}, u32[]{:S(2)}) copy-start(f32[4,8,128]{2,1,0:T(8,128)} %param.6) | copy-start | bytes 49156
  314.8 152.3 %all-to-all-start.4 = ((f32[32,8,128]{2,1,0:T(8,128)}), f32[32,8,128]{2,1,0:T(8,128)S(1)}, u32[]{:S(2)}, u32[]{:S(2)}) async-start(f32[32,8,128]{2,1,0:T(8,128)} %copy.99), calls=%async_computation.4 | async-start | bytes 262144 | tf_op jit(solution)/shard_map/all_to_all | solution.py:37
  883.8 68.7 %copy-start.3 = (f32[1,8,256]{2,1,0:T(8,128)}, f32[1,8,256]{2,1,0:T(8,128)S(1)}, u32[]{:S(2)}) copy-start(f32[1,8,256]{2,1,0:T(8,128)S(1)} %fusion.60) | copy-start | bytes 24580
  965.5 153.2 %all-to-all-start.9 = ((f32[32,8,128]{2,1,0:T(8,128)}), f32[32,8,128]{2,1,0:T(8,128)S(1)}, u32[]{:S(2)}, u32[]{:S(2)}) async-start(f32[32,8,128]{2,1,0:T(8,128)} %copy.110), calls=%async_computation.9 | async-start | bytes 262144 | tf_op jit(solution)/shard_map/all_to_all | solution.py:37
